TPU v7x, 256 devices: a whole 4x4x8 slice. The times are simulated.
256 devices in a mesh: blk: 32 (over z, x_lo, core), head: 8 (over x_hi, y).
Axes of the slice: x: 4 (x_hi: 2, x_lo: 2; x = x_hi * 2 + x_lo), y: 4, z: 8, core: 2. Of those that a mesh axis runs over, the one named last changes fastest.
Arguments:
- query_tokens: bfloat16 [16384, 3072], P(('blk', 'head')), may hold values from -12 to 12
- key_tokens: bfloat16 [16384, 3072], P(('blk', 'head')), may hold values from -6 to 6
- value_tokens: bfloat16 [16384, 3072], P(('blk', 'head')), may hold values from -6 to 6
- out_weight: bfloat16 [3072, 3072], P('head'), may hold values from -1.75 to 1.75
- kv_blocks: int32 [128, 16], P('blk'), may hold values from -1 to 127, as said below
Outputs:
- projected: bfloat16 [16384, 3072], P(('blk', 'head'))
Inputs may be any that keep to these rules, and one draw needn't show every extreme that they name: `kv_blocks`: row i lists the key blocks of 128 tokens that query block i attends to; let G = floor(i / 4). Entry 0 is i. Entry 1 is one of the blocks 4 * M to 4 * M + 3 with M = (G + 16) mod 32. Entry j >= 2 is -1 (absent) or one of the blocks 4 * (G + o) to 4 * (G + o) + 3, with o = j // 2 for even j and o = -(j - 1) // 2 for odd j; it is present whenever j < 8 and those blocks exist. Entries of one row are distinct.
All inputs are finite; a program needn't handle non-finite values.
Results may differ from a plain program's by a relative error of at most 0.012.
Values may be sent and summed in bfloat16 or wider, within the bound.
A program may use at most 128 MiB of HBM per device.

v0:
```python
import math

import jax
import jax.numpy as jnp
from jax import lax
from jax.sharding import PartitionSpec as P

HD = 128


masked_low = -1e30


def sparse_attend(query_sets, key_sets, value_sets, present):
    blocks_dev = present.shape[0]
    slots = present.shape[1]
    block_rows = query_sets.shape[2]
    scaling = 1.0 / math.sqrt(HD)
    allowed = jnp.broadcast_to(present[:, :, None], (blocks_dev, slots, block_rows)).reshape(
        blocks_dev, slots * block_rows
    )
    scores = (
        jnp.einsum("hbqd,hbkd->hbqk", query_sets, key_sets, preferred_element_type=jnp.float32)
        * scaling
    )
    mask_full = allowed[None, :, None, :]
    peak_value = jnp.max(jnp.where(mask_full, scores, masked_low), axis=-1, keepdims=True)
    weights = jnp.where(mask_full, jnp.exp(scores - peak_value), 0.0)
    denom = jnp.sum(weights, axis=-1)
    outputs = jnp.einsum(
        "hbqk,hbkd->hbqd",
        weights.astype(jnp.bfloat16),
        value_sets,
        preferred_element_type=jnp.float32,
    )
    return outputs / denom[..., None]


def on_device(query_tokens, key_tokens, value_tokens, out_weight, kv_blocks):
    queries, key_rows, value_rows = (
        lax.all_to_all(query_tokens, "head", split_axis=1, concat_axis=0, tiled=True),
        lax.all_to_all(key_tokens, "head", split_axis=1, concat_axis=0, tiled=True),
        lax.all_to_all(value_tokens, "head", split_axis=1, concat_axis=0, tiled=True),
    )
    row_total = queries.shape[0]
    feature_width = queries.shape[1]
    heads_dev = feature_width // HD
    blocks_dev = kv_blocks.shape[0]
    block_rows = row_total // blocks_dev
    slots = kv_blocks.shape[1]
    query_heads = queries.reshape(row_total, heads_dev, HD).transpose(1, 0, 2)
    query_sets = query_heads.reshape(heads_dev, blocks_dev, block_rows, HD)
    key_heads = key_rows.reshape(row_total, heads_dev, HD).transpose(1, 0, 2)
    value_heads = value_rows.reshape(row_total, heads_dev, HD).transpose(1, 0, 2)
    present = kv_blocks >= 0
    safe_index = jnp.maximum(kv_blocks, 0)
    gathered_keys, gathered_values = (
        lax.all_gather(key_heads, "blk", axis=1, tiled=True),
        lax.all_gather(value_heads, "blk", axis=1, tiled=True),
    )
    total_blocks = gathered_keys.shape[1] // block_rows
    source_keys = gathered_keys.reshape(heads_dev, total_blocks, block_rows, HD)
    source_values = gathered_values.reshape(heads_dev, total_blocks, block_rows, HD)
    flat_index = safe_index.reshape(blocks_dev * slots)
    key_sets = jnp.take(source_keys, flat_index, axis=1).reshape(
        heads_dev, blocks_dev, slots * block_rows, HD
    )
    value_sets = jnp.take(source_values, flat_index, axis=1).reshape(
        heads_dev, blocks_dev, slots * block_rows, HD
    )
    outputs = sparse_attend(query_sets, key_sets, value_sets, present)
    attended = (
        outputs.reshape(heads_dev, row_total, HD)
        .transpose(1, 0, 2)
        .reshape(row_total, feature_width)
    )
    attended = attended.astype(jnp.bfloat16)
    return lax.psum_scatter(
        jnp.dot(attended, out_weight, preferred_element_type=jnp.float32).astype(jnp.bfloat16),
        "head",
        scatter_dimension=0,
        tiled=True,
    )


def solution(mesh):
    placed = (
        P(("blk", "head"), None),
        P(("blk", "head"), None),
        P(("blk", "head"), None),
        P("head", None),
        P("blk", None),
    )
    return jax.shard_map(
        on_device, mesh=mesh, in_specs=placed, out_specs=P(("blk", "head"), None), check_vma=False
    )
```

profile of v0, /device:TPU:32, one launch (start us, length us, event | category | flops | bytes accessed | tf_op | source)
XLA Modules:
  0.0 322.1 jit_solution(16858350131159604797)
XLA Ops:
  6.5 0.0 copy-start
  6.5 0.0 copy-start.1
  6.5 0.0 all-gather.3.cloned.1.call-start
  6.5 1.2 copy.46
  7.7 16.9 %all_to_all.48 = bf16[64,8,384]{2,0,1:T(8,128)(2,1)S(1)} all-to-all(bf16[64,8,384]{2,0,1:T(8,128)(2,1)S(1)} %bitcast.64), channel_id=1, replica_groups=mesh['blk'=32,'head'=8] {'head'}, dimensions={1} | all-to-all | bytes 786432 | tf_op jit(solution)/shard_map/all_to_all | solution.py:42
  24.7 0.1 reshape.52
  24.8 0.8 copy.26
  25.6 0.0 all-gather.3.cloned.1.call-update
  25.6 0.0 all-gather.5.cloned.1.call-start
  25.6 1.0 copy.44
  26.7 12.0 %all_to_all.49 = bf16[64,8,384]{2,0,1:T(8,128)(2,1)S(1)} all-to-all(bf16[64,8,384]{2,0,1:T(8,128)(2,1)S(1)} %bitcast.65), channel_id=1, replica_groups=mesh['blk'=32,'head'=8] {'head'}, dimensions={1} | all-to-all | bytes 786432 | tf_op jit(solution)/shard_map/all_to_all | solution.py:43
  38.7 0.1 reshape.58
  38.8 0.8 copy.31
  39.7 0.0 all-gather.5.cloned.1.call-update
  39.7 1.9 copy.45
  41.5 3.5 %all-to-all-start.1 = ((bf16[64,8,384]{2,0,1:T(8,128)(2,1)}), bf16[64,8,384]{2,0,1:T(8,128)(2,1)S(1)}, u32[]{:S(2)}, u32[]{:S(2)}) async-start(bf16[64,8,384]{2,0,1:T(8,128)(2,1)} %bitcast.51), calls=%async_computation.1 | async-start | bytes 786432 | tf_op jit(solution)/shard_map/all_to_all | solution.py:41
  45.0 0.0 reduce-scatter.2.cloned.1.call-start
  45.1 0.0 copy-done.1
  45.1 0.1 reshape.54
  45.2 0.1 broadcast_bitcast_fusion
  45.3 8.9 %all-to-all-done.1 = bf16[64,8,384]{2,0,1:T(8,128)(2,1)S(1)} async-done(((bf16[64,8,384]{2,0,1:T(8,128)(2,1)}), bf16[64,8,384]{2,0,1:T(8,128)(2,1)S(1)}, u32[]{:S(2)}, u32[]{:S(2)}) %all-to-all-start.1) | async-done | bytes 393248 | tf_op jit(solution)/shard_map/all_to_all | solution.py:41
  54.2 0.1 reshape.56
  54.3 0.1 copy.29
  54.4 51.7 %all-gather.3.cloned.1.call-done = bf16[3,16384,128]{2,1,0:T(8,128)(2,1)} async-done(((bf16[3,512,128]{2,1,0:T(8,128)(2,1)}), bf16[3,16384,128]{2,1,0:T(8,128)(2,1)}) %all-gather.3.cloned.1.call-update) | async-done | bytes 12582928 | tf_op jit(solution)/shard_map/all_gather | solution.py:58
  106.1 8.6 %gather_fusion = bf16[64,3,128,128]{3,2,1,0:T(8,128)(2,1)} fusion(bf16[3,128,128,128]{3,2,1,0:T(8,128)(2,1)} %bitcast.56, s32[1024]{0:T(1024)S(1)} %pad_clamp_fusion), kind=kCustom, calls=%fused_computation.clone | custom fusion | bytes 12583168 | tf_op jit(solution)/shard_map/jit(_take)/gather | solution.py:65
  114.7 72.9 %all-gather.5.cloned.1.call-done = bf16[3,16384,128]{2,1,0:T(8,128)(2,1)} async-done(((bf16[3,512,128]{2,1,0:T(8,128)(2,1)}), bf16[3,16384,128]{2,1,0:T(8,128)(2,1)}) %all-gather.5.cloned.1.call-update) | async-done | bytes 12582928 | tf_op jit(solution)/shard_map/all_gather | solution.py:59
  187.6 8.5 %gather_fusion.1 = bf16[64,3,128,128]{3,2,1,0:T(8,128)(2,1)} fusion(bf16[3,128,128,128]{3,2,1,0:T(8,128)(2,1)} %bitcast.57, s32[1024]{0:T(1024)S(1)} %pad_clamp_fusion), kind=kCustom, calls=%fused_computation.1.clone | custom fusion | bytes 12583168 | tf_op jit(solution)/shard_map/jit(_take)/gather | solution.py:68
  196.1 5.5 %select_bitcast_fusion.1 = (bf16[3,64,128,128]{3,2,0,1:T(8,128)(2,1)S(1)}, bf16[3,64,128,128]{3,2,0,1:T(8,128)(2,1)S(1)}) fusion(bf16[64,3,128,128]{3,2,1,0:T(8,128)(2,1)} %gather_fusion, pred[64]{0:T(512)(128)(4,1)S(1)} %compare_and_fusion, bf16[64,3,128,128]{3,2,1,0:T(8,128)(2,1)} %gather_fusion.1), kind=kLoop, calls=%fused_computation.11 | loop fusion | flops 6291456 | bytes 25165888 | tf_op jit(solution)/shard_map/jit(_take)/select_n | solution.py:65
  201.7 4.0 %copy.27 = bf16[3,64,128,128]{3,2,1,0:T(8,128)(2,1)} copy(bf16[3,64,128,128]{3,2,0,1:T(8,128)(2,1)S(1)} %get-tuple-element.6) | data formatting | bytes 12582912 | tf_op jit(solution)/shard_map/jit(_take)/select_n | solution.py:65
  205.7 4.0 %copy.32 = bf16[3,64,128,128]{3,2,1,0:T(8,128)(2,1)} copy(bf16[3,64,128,128]{3,2,0,1:T(8,128)(2,1)S(1)} %get-tuple-element.7) | data formatting | bytes 12582912 | tf_op jit(solution)/shard_map/jit(_take)/select_n | solution.py:68
  209.7 10.3 %bitcast_reduce_fusion = (f32[3,4,128]{2,1,0:T(4,128)S(1)}, bf16[3,4,2048,128]{3,2,1,0:T(8,128)(2,1)}) fusion(pred[4,2048]{1,0:T(4,128)(4,1)S(1)} %bitcast.72, bf16[3,4,2048,128]{3,2,1,0:T(8,128)(2,1)} %bitcast.54, bf16[3,4,128,128]{3,2,1,0:T(8,128)(2,1)S(1)} %bitcast.66), kind=kOutput, calls=%fused_computation.3 | convolution fusion | flops 1632634880 | bytes 12990464 | tf_op jit(solution)/shard_map/sub | solution.py:28
  220.0 6.6 %fusion.10 = bf16[3,4,128,128]{3,2,1,0:T(8,128)(2,1)S(1)} fusion(bf16[3,4,2048,128]{3,2,1,0:T(8,128)(2,1)} %bitcast.55, f32[3,4,128]{2,1,0:T(4,128)S(1)} %get-tuple-element.8, bf16[3,4,2048,128]{3,2,1,0:T(8,128)(2,1)} %get-tuple-element.9), kind=kOutput, calls=%fused_computation.17 | convolution fusion | flops 805699584 | bytes 12982272 | tf_op jit(solution)/shard_map/hbqk,hbkd->hbqd/dot_general | solution.py:30
  226.7 0.2 copy.34
  226.9 0.0 copy-done
  226.9 3.5 %convolution_convert_fusion = bf16[512,3072]{1,0:T(8,128)(2,1)} fusion(bf16[512,384]{0,1:T(8,128)(2,1)S(1)} %bitcast.71, bf16[384,3072]{1,0:T(8,128)(2,1)S(1)} %copy-done), kind=kOutput, calls=%fused_computation.15 | convolution fusion | flops 1209532416 | bytes 5898240 | tf_op jit(solution)/shard_map/dot_general | solution.py:79
  230.3 0.0 reduce-scatter.2.cloned.1.call-update
  230.4 85.2 %reduce-scatter.2.cloned.1.call-done = bf16[64,3072]{1,0:T(8,128)(2,1)} async-done(((bf16[512,3072]{1,0:T(8,128)(2,1)}), bf16[64,3072]{1,0:T(8,128)(2,1)}) %reduce-scatter.2.cloned.1.call-update) | async-done | bytes 393232 | tf_op jit(solution)/shard_map/reduce_scatter | solution.py:78
  (6 shorter events, 0.0 us)
Async XLA Ops:
  6.5 220.3 %copy-start = (bf16[384,3072]{1,0:T(8,128)(2,1)S(1)}, bf16[384,3072]{1,0:T(8,128)(2,1)}, u32[]{:S(2)}) copy-start(bf16[384,3072]{1,0:T(8,128)(2,1)} %param.10) | copy-start | bytes 7077892
  6.5 38.5 %copy-start.1 = (s32[4,16]{1,0:T(4,128)S(1)}, s32[4,16]{1,0:T(4,128)}, u32[]{:S(2)}) copy-start(s32[4,16]{1,0:T(4,128)} %param.11) | copy-start | bytes 772
  6.5 99.5 %all-gather.3.cloned.1.call-start = ((), (), s32[]{:S(2)}) async-start(), calls=%async_computation.4 | async-start | bytes 12976128 | tf_op jit(solution)/shard_map/all_gather | solution.py:58
  25.6 162.0 %all-gather.5.cloned.1.call-start = ((), (), s32[]{:S(2)}) async-start(), calls=%async_computation.5 | async-start | bytes 12976128 | tf_op jit(solution)/shard_map/all_gather | solution.py:59
  41.5 12.6 %all-to-all-start.1 = ((bf16[64,8,384]{2,0,1:T(8,128)(2,1)}), bf16[64,8,384]{2,0,1:T(8,128)(2,1)S(1)}, u32[]{:S(2)}, u32[]{:S(2)}) async-start(bf16[64,8,384]{2,0,1:T(8,128)(2,1)} %bitcast.51), calls=%async_computation.1 | async-start | bytes 786432 | tf_op jit(solution)/shard_map/all_to_all | solution.py:41
  45.0 270.6 %reduce-scatter.2.cloned.1.call-start = ((), (), s32[]{:S(2)}) async-start(), calls=%async_computation.6 | async-start | bytes 3538944 | tf_op jit(solution)/shard_map/reduce_scatter | solution.py:78
Sparse Core Ops, SparseCore 0:
  25.7 80.2 all-gather.2
  107.9 79.6 all-gather.4
  230.5 85.0 reduce-scatter.1
where the time goes:
time: 323 us; the launch traced here: 322 us
  waiting for transfers between devices  219 us (68%)
  local copies, waits for them, and re-layouts  31.7 us (10%)
  blocking collectives  28.9 us (9%)
  matrix products  20.4 us (6%)
  between operations  13.2 us (4%)
  other arithmetic  5.58 us (2%)
  starting transfers between devices  3.54 us (1%)
    reduce_scatter x1, waiting for transfers between devices, on_device(): lax.psum_scatter(jnp.dot(attended, out_weight, preferred_element_type=jnp...  85.2 us
    all_gather x1, waiting for transfers between devices, on_device(): lax.all_gather(value_heads, 'blk', axis=1, tiled=True)  72.9 us
    all_gather x1, waiting for transfers between devices, on_device(): lax.all_gather(key_heads, 'blk', axis=1, tiled=True)  51.7 us
    all_to_all x1, blocking collectives, on_device(): lax.all_to_all(key_tokens, 'head', split_axis=1, concat_axis=0, tiled=True)  16.9 us
    all_to_all x1, blocking collectives, on_device(): lax.all_to_all(value_tokens, 'head', split_axis=1, concat_axis=0, tiled=T...  12 us
    sub x1, matrix products, sparse_attend(): weights = jnp.where(mask_full, jnp.exp(scores - peak_value), 0.0)  10.3 us
    all_to_all x1, waiting for transfers between devices, on_device(): lax.all_to_all(query_tokens, 'head', split_axis=1, concat_axis=0, tiled=T...  8.89 us
    gather x1, local copies, waits for them, and re-layouts, on_device(): jnp.take(source_keys, flat_index, axis=1)  8.63 us
  transfers between devices with their start and end apart: 4, of which 4 were waited for; matrix products, arithmetic and copies ran while one was open for 4% of the time, Pallas kernels for 0%

commit v1 on v0

v1 whole, which is shorter than its diff:
```python
import functools
import math

import jax
import jax.numpy as jnp
from jax import lax
from jax.experimental import pallas as pl
from jax.experimental.pallas import tpu as pltpu
from jax.sharding import PartitionSpec as P

HD = 128
BLOCK = 128
VM = pltpu.VMEM
F32 = jnp.float32
BF16 = jnp.bfloat16


def greet(n):
    me = lax.axis_index("head")
    barrier = pltpu.get_barrier_semaphore()
    for k in range(1, n):
        pl.semaphore_signal(barrier, inc=1, device_id={"head": lax.rem(me + k, n)})
    pl.semaphore_wait(barrier, n - 1)
    return me


def spread_kernel(n, q_ref, k_ref, v_ref, qo_ref, kvo_ref, send_sem, recv_sem, own_sem):
    rows = q_ref.shape[0]
    width = q_ref.shape[1] // n
    me = greet(n)
    here = pl.ds(pl.multiple_of(me * rows, rows), rows)

    def pieces(dest):
        cols = pl.ds(pl.multiple_of(dest * width, width), width)
        return (
            (k_ref.at[:, cols], kvo_ref.at[here, pl.ds(0, width)]),
            (v_ref.at[:, cols], kvo_ref.at[here, pl.ds(width, width)]),
            (q_ref.at[:, cols], qo_ref.at[here, :]),
        )

    copies = []
    for k in range(1, n):
        dest = lax.rem(me + k, n)
        for a, (src, dst) in enumerate(pieces(dest)):
            c = pltpu.make_async_remote_copy(
                src, dst, send_sem.at[k - 1, a], recv_sem.at[k - 1, a], device_id={"head": dest}
            )
            c.start()
            copies.append(c)
    own = []
    for a, (src, dst) in enumerate(pieces(me)):
        c = pltpu.make_async_copy(src, dst, own_sem.at[a])
        c.start()
        own.append(c)
    for c in own:
        c.wait()
    for c in copies:
        c.wait()


def spread(n, q, k, v):
    rows, full = q.shape
    width = full // n
    whole = pl.BlockSpec(memory_space=VM)
    return pl.pallas_call(
        functools.partial(spread_kernel, n),
        out_shape=(
            jax.ShapeDtypeStruct((rows * n, width), BF16),
            jax.ShapeDtypeStruct((rows * n, 2 * width), BF16),
        ),
        in_specs=[whole] * 3,
        out_specs=(whole, whole),
        scratch_shapes=[
            pltpu.SemaphoreType.DMA((n - 1, 3)),
            pltpu.SemaphoreType.DMA((n - 1, 3)),
            pltpu.SemaphoreType.DMA((3,)),
        ],
        compiler_params=pltpu.CompilerParams(collective_id=0, has_side_effects=True),
    )(q, k, v)


def reduce_kernel(n, x_ref, o_ref, held, send_sem, recv_sem):
    rows = o_ref.shape[0]
    me = greet(n)
    copies = []
    for k in range(1, n):
        dest = lax.rem(me + k, n)
        c = pltpu.make_async_remote_copy(
            x_ref.at[pl.ds(pl.multiple_of(dest * rows, rows), rows), :],
            held.at[k - 1],
            send_sem.at[k - 1],
            recv_sem.at[k - 1],
            device_id={"head": dest},
        )
        c.start()
        copies.append(c)
    for c in copies:
        c.wait()
    mine = pl.ds(pl.multiple_of(me * rows, rows), rows)
    step = 512

    def add(i, carry):
        cols = pl.ds(pl.multiple_of(i * step, step), step)
        total = x_ref[mine, cols].astype(F32)
        for k in range(n - 1):
            total = total + held[k, :, cols].astype(F32)
        o_ref[:, cols] = total.astype(BF16)
        return carry

    lax.fori_loop(0, o_ref.shape[1] // step, add, 0)


def reduce_rows(n, x):
    rows = x.shape[0] // n
    whole = pl.BlockSpec(memory_space=VM)
    return pl.pallas_call(
        functools.partial(reduce_kernel, n),
        out_shape=jax.ShapeDtypeStruct((rows, x.shape[1]), BF16),
        in_specs=[whole],
        out_specs=whole,
        scratch_shapes=[
            VM((n - 1, rows, x.shape[1]), BF16),
            pltpu.SemaphoreType.DMA((n - 1,)),
            pltpu.SemaphoreType.DMA((n - 1,)),
        ],
        compiler_params=pltpu.CompilerParams(collective_id=1, has_side_effects=True),
    )(x)


def attend_kernel(slots, heads, index_ref, q_ref, bias_ref, *refs):
    ks, vs = refs[:slots], refs[slots : 2 * slots]
    w_ref, o_ref = refs[2 * slots], refs[2 * slots + 1]
    scaling = 1.0 / math.sqrt(HD)
    done = []
    for h in range(heads):
        cols = slice(h * HD, (h + 1) * HD)
        keys = jnp.concatenate([r[:, cols] for r in ks], axis=0)
        values = jnp.concatenate([r[:, cols] for r in vs], axis=0)
        scores = lax.dot_general(
            q_ref[:, cols], keys, (((1,), (1,)), ((), ())), preferred_element_type=F32
        )
        scores = scores * scaling + bias_ref[0]
        peak = jnp.max(scores, axis=-1, keepdims=True)
        weights = jnp.exp(scores - peak)
        denom = jnp.sum(weights, axis=-1, keepdims=True)
        out = jnp.dot(weights.astype(BF16), values, preferred_element_type=F32)
        done.append((out / denom).astype(BF16))
    attended = jnp.concatenate(done, axis=1)
    o_ref[...] = jnp.dot(attended, w_ref[...], preferred_element_type=F32).astype(BF16)


def attend(queries, kv, weight, kv_blocks):
    blocks, slots = kv_blocks.shape
    width = queries.shape[1]
    heads = width // HD
    bias = jnp.where(kv_blocks >= 0, 0.0, -1e30).astype(F32)
    bias = jnp.repeat(bias, BLOCK, axis=1).reshape(blocks, 1, slots * BLOCK)
    index = jnp.maximum(kv_blocks, 0)

    def side(j, half):
        return pl.BlockSpec((BLOCK, width), lambda i, idx: (idx[i, j], half))

    return pl.pallas_call(
        functools.partial(attend_kernel, slots, heads),
        out_shape=jax.ShapeDtypeStruct((queries.shape[0], weight.shape[1]), BF16),
        grid_spec=pltpu.PrefetchScalarGridSpec(
            num_scalar_prefetch=1,
            grid=(blocks,),
            in_specs=[
                pl.BlockSpec((BLOCK, width), lambda i, idx: (i, 0)),
                pl.BlockSpec((1, 1, slots * BLOCK), lambda i, idx: (i, 0, 0)),
            ]
            + [side(j, 0) for j in range(slots)]
            + [side(j, 1) for j in range(slots)]
            + [pl.BlockSpec(weight.shape, lambda i, idx: (0, 0))],
            out_specs=pl.BlockSpec((BLOCK, weight.shape[1]), lambda i, idx: (i, 0)),
        ),
        compiler_params=pltpu.CompilerParams(vmem_limit_bytes=48 << 20),
    )(index, queries, bias, *([kv] * (2 * slots)), weight)


def on_device(n, query_tokens, key_tokens, value_tokens, out_weight, kv_blocks):
    queries, kv = spread(n, query_tokens, key_tokens, value_tokens)
    gathered = lax.all_gather(kv, "blk", axis=0, tiled=True)
    partial = attend(queries, gathered, out_weight, kv_blocks)
    return reduce_rows(n, partial)


def solution(mesh):
    placed = (
        P(("blk", "head"), None),
        P(("blk", "head"), None),
        P(("blk", "head"), None),
        P("head", None),
        P("blk", None),
    )
    return jax.shard_map(
        functools.partial(on_device, mesh.shape["head"]),
        mesh=mesh,
        in_specs=placed,
        out_specs=P(("blk", "head"), None),
        check_vma=False,
    )
```

time: 323 us -> 259 us (0.80)
  Pallas kernels: 0 us -> 89.6 us
  waiting for transfers between devices: 219 us -> 144 us
  blocking collectives: 28.9 us -> 0 us
  local copies, waits for them, and re-layouts: 31.7 us -> 6.15 us
  matrix products: 20.4 us -> 0 us
  other arithmetic: 5.58 us -> 1.37 us
  starting transfers between devices: 3.54 us -> 0.01 us
    pallas_call x0 -> x3, Pallas kernels: none -> 89.6 us  [the longest x1 53.3 us: reduce_rows(): pl.pallas_call(functools.partial(reduce_kernel, n), out_shape=jax.ShapeDt...]
    reduce_scatter x1 -> x0, waiting for transfers between devices: 85.2 us -> none  [on_device(): lax.psum_scatter(jnp.dot(attended, out_weight, preferred_element_type=jnp...]
    all_to_all x2 -> x0, blocking collectives: 28.9 us -> none  [the longest x1 16.9 us: on_device(): lax.all_to_all(key_tokens, 'head', split_axis=1, concat_axis=0, tiled=True)]
    all_gather x2 -> x1, waiting for transfers between devices: 125 us -> 144 us  [on_device(): gathered = lax.all_gather(kv, 'blk', axis=0, tiled=True)]
    gather x2 -> x0, local copies, waits for them, and re-layouts: 17.2 us -> none  [the longest x1 8.63 us: on_device(): jnp.take(source_keys, flat_index, axis=1)]
    sub x1 -> x0, matrix products: 10.3 us -> none  [sparse_attend(): weights = jnp.where(mask_full, jnp.exp(scores - peak_value), 0.0)]
    dot_general x2 -> x0, matrix products: 10.1 us -> none  [the longest x1 6.63 us: sparse_attend(): jnp.einsum('hbqk,hbkd->hbqd', weights.astype(jnp.bfloat16), value_sets, p...]
    all_to_all x1 -> x0, waiting for transfers between devices: 8.89 us -> none  [on_device(): lax.all_to_all(query_tokens, 'head', split_axis=1, concat_axis=0, tiled=T...]
  transfers between devices with their start and end apart: 4 -> 1, of which waited for: 4 -> 1; matrix products, arithmetic and copies ran while one was open for 4% -> 1% of each run, Pallas kernels for 0% -> 0%
where the time goes in v1:
time: 259 us; the launch traced here: 255 us
  waiting for transfers between devices  144 us (56%)
  Pallas kernels  89.6 us (35%)
  between operations  13.4 us (5%)
  local copies, waits for them, and re-layouts  6.15 us (2%)
    all_gather x1, waiting for transfers between devices, on_device(): gathered = lax.all_gather(kv, 'blk', axis=0, tiled=True)  144 us
    pallas_call x1, Pallas kernels, reduce_rows(): pl.pallas_call(functools.partial(reduce_kernel, n), out_shape=jax.ShapeDt...  53.3 us
    pallas_call x1, Pallas kernels, spread(): pl.pallas_call(functools.partial(spread_kernel, n), out_shape=(jax.ShapeD...  22.5 us
    pallas_call x1, Pallas kernels, attend(): pl.pallas_call(functools.partial(attend_kernel, slots, heads), out_shape=...  13.8 us
    unnamed x7, local copies, waits for them, and re-layouts  6.08 us
  transfers between devices with their start and end apart: 1, of which 1 were waited for; matrix products, arithmetic and copies ran while one was open for 1% of the time, Pallas kernels for 0%

profile of v1, /device:TPU:32, one launch (start us, length us, event | category | flops | bytes accessed | tf_op | source)
XLA Modules:
  0.0 254.9 jit_solution(12944066894252304729)
XLA Ops:
  6.5 0.0 all-gather.2.cloned.1.call-start
  6.5 22.5 %shard_map.55 = (bf16[512,384]{1,0:T(8,128)(2,1)}, bf16[512,768]{1,0:T(8,128)(2,1)}) custom-call(bf16[64,3072]{1,0:T(8,128)(2,1)} %q_ref.1, bf16[64,3072]{1,0:T(8,128)(2,1)} %k_ref.1, bf16[64,3072]{1,0:T(8,128)(2,1)} %v_ref.1), custom_call_target="tpu_custom_call" | custom-call | tf_op jit(solution)/shard_map/pallas_call | solution.py:65
  29.1 0.0 all-gather.2.cloned.1.call-update
  29.1 0.7 compare_select_fusion
  29.8 0.7 broadcast_maximum_fusion.index_ref
  30.4 144.3 %all-gather.2.cloned.1.call-done.refs_0_.refs_1_.refs_2_.refs_3_.refs_4_.refs_5_.refs_6_.refs_7_.refs_8_.refs_9_.refs_10_.refs_11_.refs_12_.refs_13_.refs_14_.refs_15_.refs_16_.refs_17_.refs_18_.refs_19_.refs_20_.refs_21_.refs_22_.refs_23_.refs_24_.refs_25_.refs_26_.refs_27_.refs_28_.refs_29_.refs_30_.refs_31_ = bf16[16384,768]{1,0:T(8,128)(2,1)} async-done(((bf16[512,768]{1,0:T(8,128)(2,1)}), ...) | async-done | bytes 25165840 | tf_op jit(solution)/shard_map/all_gather | solution.py:184
  174.8 0.1 broadcast_in_dim.13
  174.9 0.0 copy-start.1
  174.9 1.7 copy-done.1
  176.5 0.0 copy-start.2
  176.5 1.0 copy-done.2
  177.5 13.8 %shard_map.56.x_ref = bf16[512,3072]{1,0:T(8,128)(2,1)S(1)} custom-call(s32[4,16]{1,0:T(4,128)S(1)} %broadcast_maximum_fusion.index_ref, bf16[512,384]{1,0:T(8,128)(2,1)S(1)} %copy-done.2, f32[4,1,2048]{2,1,0:T(1,128)S(1)} %bitcast.1, ...), custom_call_target="tpu_custom_call" | custom-call | tf_op jit(solution)/shard_map/pallas_call | solution.py:163
  191.4 0.0 copy-start
  191.4 1.6 copy-done
  193.0 53.3 %shard_map.57 = bf16[64,3072]{1,0:T(8,128)(2,1)} custom-call(bf16[512,3072]{1,0:T(8,128)(2,1)} %copy-done), custom_call_target="tpu_custom_call" | custom-call | tf_op jit(solution)/shard_map/pallas_call | solution.py:116
  246.3 1.8 copy.7
Async XLA Ops:
  6.5 168.3 %all-gather.2.cloned.1.call-start = ((), (), s32[]{:S(2)}) async-start(), calls=%async_computation | async-start | bytes 25952256 | tf_op jit(solution)/shard_map/all_gather | solution.py:184
  174.9 1.7 copy-start.1
  176.5 1.0 copy-start.2
  191.4 1.7 copy-start
Sparse Core Ops, SparseCore 0:
  29.2 145.5 all-gather.1
